TPU v7x, 32 devices: a whole 2x2x4 slice. The times are simulated.
32 devices in a mesh: dp: 8 (over y, x, core), mp: 4 (over z).
Axes of the slice: x: 2, y: 2, z: 4, core: 2. Of those that a mesh axis runs over, the one named last changes fastest.
Arguments:
- tokens_in: bfloat16 [1024, 5120], P('dp'), may hold values from -6 to 6
- cotangent: bfloat16 [1024, 10240], P('dp', 'mp'), may hold values from -6 to 6
- old_weights: bfloat16 [112, 128, 128], P('mp'), may hold values from -0.25 to 0.25
- old_first: float32 [112, 16384], P('mp', 'dp'), may hold values from -6 to 6
- old_second: float32 [112, 16384], P('mp', 'dp'), may hold values from 0.25 to 4
- new_coords: int32 [80, 2], replicated, may hold values from 0 to 79, as said below
- moved_to: int32 [112], replicated, may hold values from -1 to 79, as said below
Outputs:
- activated: bfloat16 [1024, 10240], P('dp', 'mp')
- input_grads: bfloat16 [1024, 5120], P('dp', 'mp')
- new_weights: bfloat16 [80, 128, 128], P('mp')
- new_first: float32 [80, 16384], P('mp', 'dp')
- new_second: float32 [80, 16384], P('mp', 'dp')
Inputs may be any that keep to these rules, and one draw needn't show every extreme that they name: new_coords[b] is (row block, column block) of new slot b, owned by mp index b // 20; no two slots share a cell. Call the column blocks of one index of mp a band; no owner has more than 11 blocks in one band, and in every draw some band holds exactly 11 blocks of every owner. moved_to[o] is the new slot that old slot o (held by mp index o // 28) moves to, or -1 where the old block is pruned or the slot is empty. Each new slot is named at most once; new slots that no old slot names are regrown. At most 7 blocks move from one old owner to one new owner; in every draw every new owner receives exactly 7 from some old owner, and some new owner receives 20 blocks in all.
All inputs are finite; a program needn't handle non-finite values.
Results may differ from a plain program's by a relative error of at most 0.0055.
Values may be sent and summed in bfloat16 or wider, within the bound.
No kernel may reach another device: no remote copies, remote signals or barrier semaphores. Data moves between devices by JAX's collectives and lax.ppermute only.
A program may use at most 64 MiB of HBM per device.

v0:
```python
import math
import jax
import jax.numpy as jnp
from jax import lax
from jax.sharding import PartitionSpec as P

BETA_ONE = 0.9
BETA_TWO = 0.95
LEARN_RATE = 0.01
ADAM_EPSILON = 0.05


def gelu_tanh(values):
    return jax.nn.gelu(values, approximate=True)


def pick_rows(source_rows, row_index, filled):
    picked = jnp.take(source_rows, row_index, axis=0)
    shape_tail = (1,) * (source_rows.ndim - 1)
    return jnp.where(filled.reshape((-1,) + shape_tail), picked, jnp.zeros_like(picked))


def inverse_slots(positions, slot_count):
    targets = jnp.arange(slot_count, dtype=jnp.int32)
    matches = positions[None, :] == targets[:, None]
    entries = jnp.arange(positions.shape[0], dtype=jnp.int32)
    source = jnp.sum(jnp.where(matches, entries[None, :], 0), axis=1)
    return (source, jnp.any(matches, axis=1))


def ranks_within(labels, label_count):
    onehot = (labels[:, :, None] == jnp.arange(label_count, dtype=jnp.int32)[None, None, :]).astype(
        jnp.int32
    )
    before = jnp.cumsum(onehot, axis=1) - onehot
    return jnp.sum(before * onehot, axis=2)


def body(tokens_in, cotangent, old_weights, old_first, old_second, new_coords, moved_to):
    owners = lax.axis_size("mp")
    replicas = lax.axis_size("dp")
    owner_here = lax.axis_index("mp")
    replica = lax.axis_index("dp")
    capacity = old_weights.shape[0]
    block_size = old_weights.shape[1]
    total_blocks = new_coords.shape[0]
    per_owner = total_blocks // owners
    shard_len = old_first.shape[1]
    token_count = tokens_in.shape[0]
    model_width = tokens_in.shape[1]
    band_width = cotangent.shape[1] // block_size
    move_slots = capacity // owners
    band_slots = 2 * per_owner // owners + 1
    dest_slot = moved_to.reshape(owners, capacity)
    dest_owner = jnp.where(dest_slot >= 0, dest_slot // per_owner, -1)
    move_rank = ranks_within(dest_owner, owners)
    here_owner = lax.dynamic_index_in_dim(dest_owner, owner_here, 0, keepdims=False)
    here_rank = lax.dynamic_index_in_dim(move_rank, owner_here, 0, keepdims=False)
    send_place = jnp.where(
        here_owner >= 0, here_owner * move_slots + here_rank, owners * move_slots
    )
    send_source, send_filled = inverse_slots(send_place, owners * move_slots)
    outgoing = pick_rows(old_weights, send_source, send_filled)
    out_first = pick_rows(old_first, send_source, send_filled)
    out_second = pick_rows(old_second, send_source, send_filled)
    arrived_weights = lax.all_to_all(outgoing, "mp", split_axis=0, concat_axis=0, tiled=True)
    arrived_first, arrived_second = (
        lax.all_to_all(out_first, "mp", split_axis=0, concat_axis=0, tiled=True),
        lax.all_to_all(out_second, "mp", split_axis=0, concat_axis=0, tiled=True),
    )
    old_owner = jnp.arange(owners * capacity, dtype=jnp.int32) // capacity
    flat_place = old_owner * move_slots + move_rank.reshape(-1)
    recv_source, recv_filled = inverse_slots(moved_to - owner_here * per_owner, per_owner)
    recv_index = jnp.take(flat_place, recv_source)
    weights_now = pick_rows(arrived_weights, recv_index, recv_filled)
    first_now = pick_rows(arrived_first, recv_index, recv_filled)
    second_now = pick_rows(arrived_second, recv_index, recv_filled)
    my_coords = lax.dynamic_slice_in_dim(new_coords, owner_here * per_owner, per_owner, 0)
    row_ids = my_coords[:, 0]
    token_blocks = jnp.take(
        tokens_in.reshape(token_count, model_width // block_size, block_size), row_ids, axis=1
    )
    products = jnp.einsum(
        "tbk,bkn->btn", token_blocks, weights_now, preferred_element_type=jnp.float32
    ).astype(jnp.bfloat16)
    all_band = new_coords[:, 1] // band_width
    band_rank = ranks_within(all_band.reshape(owners, per_owner), owners).reshape(-1)
    my_band = lax.dynamic_slice_in_dim(all_band, owner_here * per_owner, per_owner, 0)
    my_rank = lax.dynamic_slice_in_dim(band_rank, owner_here * per_owner, per_owner, 0)
    out_place = my_band * band_slots + my_rank
    out_source, out_filled = inverse_slots(out_place, owners * band_slots)
    outgoing_products = pick_rows(products, out_source, out_filled)
    arrived_products = lax.all_to_all(
        outgoing_products, "mp", split_axis=0, concat_axis=0, tiled=True
    )
    all_owner = jnp.arange(total_blocks, dtype=jnp.int32) // per_owner
    incoming_key = jnp.where(all_band == owner_here, all_owner * band_slots + band_rank, -1)
    local_col = new_coords[:, 1] - owner_here * band_width
    key_match = (
        incoming_key[None, :] == jnp.arange(owners * band_slots, dtype=jnp.int32)[:, None]
    ).astype(jnp.float32)
    col_match = (local_col[:, None] == jnp.arange(band_width, dtype=jnp.int32)[None, :]).astype(
        jnp.float32
    )
    placement = jnp.dot(key_match, col_match).astype(jnp.bfloat16)
    hidden = jnp.einsum(
        "qc,qtn->tcn", placement, arrived_products, preferred_element_type=jnp.float32
    )
    hidden = hidden.reshape(token_count, band_width * block_size)
    activated = gelu_tanh(hidden).astype(jnp.bfloat16)
    pullback = jax.vjp(gelu_tanh, hidden)[1]
    slopes = pullback(cotangent.astype(jnp.float32))[0].astype(jnp.bfloat16)
    band_slopes = slopes.reshape(token_count, band_width, block_size)
    outgoing_slopes = jnp.einsum(
        "qc,tcn->qtn", placement, band_slopes, preferred_element_type=jnp.float32
    ).astype(jnp.bfloat16)
    arrived_slopes = lax.all_to_all(outgoing_slopes, "mp", split_axis=0, concat_axis=0, tiled=True)
    slope_blocks = jnp.take(arrived_slopes, out_place, axis=0)
    slope_form = "btn"
    block_grads = jnp.einsum(
        "tbk," + slope_form + "->bkn",
        token_blocks,
        slope_blocks,
        preferred_element_type=jnp.float32,
    )
    back_terms = jnp.einsum(
        slope_form + ",bkn->tbk", slope_blocks, weights_now, preferred_element_type=jnp.float32
    )
    input_terms = jnp.zeros((token_count, model_width // block_size, block_size), jnp.float32)
    input_terms = input_terms.at[:, row_ids, :].add(back_terms)
    input_terms = input_terms.reshape(token_count, model_width)
    grad_inputs = lax.psum_scatter(input_terms, "mp", scatter_dimension=1, tiled=True).astype(
        jnp.bfloat16
    )
    flat_grads = block_grads.reshape(per_owner, block_size * block_size)
    summed = lax.psum(flat_grads.astype(jnp.bfloat16), "dp").astype(jnp.float32)
    grad_share = lax.dynamic_slice_in_dim(summed, replica * shard_len, shard_len, 1)
    grad_share = grad_share * (1.0 / math.sqrt(token_count * replicas))
    first_new = BETA_ONE * first_now + (1.0 - BETA_ONE) * grad_share
    second_new = BETA_TWO * second_now + (1.0 - BETA_TWO) * grad_share * grad_share
    flat_weights = weights_now.reshape(per_owner, block_size * block_size)
    weight_share = lax.dynamic_slice_in_dim(flat_weights, replica * shard_len, shard_len, 1).astype(
        jnp.float32
    )
    weight_next = (
        weight_share - LEARN_RATE * first_new / (jnp.sqrt(second_new) + ADAM_EPSILON)
    ).astype(jnp.bfloat16)
    weights_out = lax.all_gather(weight_next, "dp", axis=1, tiled=True).reshape(
        per_owner, block_size, block_size
    )
    return (activated, grad_inputs, weights_out, first_new, second_new)


def solution(mesh):
    in_specs = (
        P("dp", None),
        P("dp", "mp"),
        P("mp", None, None),
        P("mp", "dp"),
        P("mp", "dp"),
        P(),
        P(),
    )
    out_specs = (P("dp", "mp"), P("dp", "mp"), P("mp", None, None), P("mp", "dp"), P("mp", "dp"))
    return jax.shard_map(body, mesh=mesh, in_specs=in_specs, out_specs=out_specs, check_vma=False)
```

profile of v0, /device:TPU:0, one launch (start us, length us, event | category | flops | bytes accessed | tf_op | source)
XLA Modules:
  0.0 213.0 jit_solution(905694268786100202)
XLA Ops:
  11.2 1.2 select_select_fusion.1
  12.3 6.5 %all-to-all-start = ((bf16[28,128,128]{2,1,0:T(8,128)(2,1)}), bf16[28,128,128]{2,1,0:T(8,128)(2,1)}, u32[]{:S(2)}, u32[]{:S(2)}) async-start(bf16[28,128,128]{2,1,0:T(8,128)(2,1)} %select_select_fusion.1), calls=%async_computation | async-start | bytes 1835008 | tf_op jit(solution)/shard_map/all_to_all | solution.py:66
  19.6 1.2 fusion.51
  26.2 1.5 gather_fusion
  28.6 13.3 %all-to-all-done = bf16[28,128,128]{2,1,0:T(8,128)(2,1)} async-done(((bf16[28,128,128]{2,1,0:T(8,128)(2,1)}), bf16[28,128,128]{2,1,0:T(8,128)(2,1)}, u32[]{:S(2)}, u32[]{:S(2)}) %all-to-all-start) | async-done | bytes 917536 | tf_op jit(solution)/shard_map/all_to_all | solution.py:66
  41.9 1.8 gather_fusion.3
  45.8 1.4 select_select_fusion
  47.2 3.5 %all-to-all-start.1 = ((bf16[44,128,128]{2,1,0:T(8,128)(2,1)}), bf16[44,128,128]{2,1,0:T(8,128)(2,1)S(1)}, u32[]{:S(2)}, u32[]{:S(2)}) async-start(bf16[44,128,128]{2,1,0:T(8,128)(2,1)} %select_select_fusion), calls=%async_computation.1 | async-start | bytes 2883584 | tf_op jit(solution)/shard_map/all_to_all | solution.py:93
  50.7 1.4 copy.51
  52.4 32.0 %all-to-all-done.1 = bf16[44,128,128]{2,1,0:T(8,128)(2,1)S(1)} async-done(((bf16[44,128,128]{2,1,0:T(8,128)(2,1)}), bf16[44,128,128]{2,1,0:T(8,128)(2,1)S(1)}, u32[]{:S(2)}, u32[]{:S(2)}) %all-to-all-start.1) | async-done | bytes 1441824 | tf_op jit(solution)/shard_map/all_to_all | solution.py:93
  84.4 2.1 fusion.2
  86.5 1.8 copy.50
  88.3 1.9 fusion.7
  91.2 1.5 copy.53
  92.7 3.7 %all-to-all-start.2 = ((bf16[44,128,128]{2,1,0:T(8,128)(2,1)}), bf16[44,128,128]{2,1,0:T(8,128)(2,1)S(1)}, u32[]{:S(2)}, u32[]{:S(2)}) async-start(bf16[44,128,128]{2,1,0:T(8,128)(2,1)} %copy.53), calls=%async_computation.2 | async-start | bytes 2883584 | tf_op jit(solution)/shard_map/all_to_all | solution.py:117
  96.5 33.6 %all-to-all-done.2 = bf16[44,128,128]{2,1,0:T(8,128)(2,1)S(1)} async-done(((bf16[44,128,128]{2,1,0:T(8,128)(2,1)}), bf16[44,128,128]{2,1,0:T(8,128)(2,1)S(1)}, u32[]{:S(2)}, u32[]{:S(2)}) %all-to-all-start.2) | async-done | bytes 1441824 | tf_op jit(solution)/shard_map/all_to_all | solution.py:117
  130.0 1.5 gather_fusion.5
  131.6 1.6 convolution_convert_fusion.1
  133.2 1.4 copy.60
  134.7 1.7 fusion.19
  136.8 4.4 %scatter_fusion = f32[128,40,128]{2,0,1:T(8,128)S(1)} fusion(f32[128,40,128]{2,0,1:T(8,128)S(1)} %broadcast_in_dim.224, s32[20]{0:T(128)S(1)} %get-tuple-element.48, f32[20,128,128]{2,1,0:T(8,128)} %fusion.19), kind=kCustom, calls=%fused_computation.10 | custom fusion | flops 327680 | bytes 3932240 | tf_op jit(solution)/shard_map/scatter-add | solution.py:130
  141.2 2.1 copy.54
  146.4 3.4 %all-to-all-start.4 = ((f32[4,7,2048]{2,1,0:T(8,128)}), f32[4,7,2048]{2,1,0:T(8,128)S(1)}, u32[]{:S(2)}, u32[]{:S(2)}) async-start(f32[4,7,2048]{2,1,0:T(8,128)} %all_to_all.31), calls=%async_computation.5 | async-start | bytes 524288 | tf_op jit(solution)/shard_map/all_to_all | solution.py:69
  150.6 15.6 %all-to-all-done.4 = f32[4,7,2048]{2,1,0:T(8,128)S(1)} async-done(((f32[4,7,2048]{2,1,0:T(8,128)}), f32[4,7,2048]{2,1,0:T(8,128)S(1)}, u32[]{:S(2)}, u32[]{:S(2)}) %all-to-all-start.4) | async-done | bytes 229408 | tf_op jit(solution)/shard_map/all_to_all | solution.py:69
  166.2 3.6 %all-to-all-start.3 = ((f32[4,7,2048]{2,1,0:T(8,128)}), f32[4,7,2048]{2,1,0:T(8,128)S(1)}, u32[]{:S(2)}, u32[]{:S(2)}) async-start(f32[4,7,2048]{2,1,0:T(8,128)} %all_to_all.28), calls=%async_computation.4 | async-start | bytes 524288 | tf_op jit(solution)/shard_map/all_to_all | solution.py:68
  170.5 16.9 %all-to-all-done.3 = f32[4,7,2048]{2,1,0:T(8,128)S(1)} async-done(((f32[4,7,2048]{2,1,0:T(8,128)}), f32[4,7,2048]{2,1,0:T(8,128)S(1)}, u32[]{:S(2)}, u32[]{:S(2)}) %all-to-all-start.3) | async-done | bytes 229408 | tf_op jit(solution)/shard_map/all_to_all | solution.py:68
  189.1 1.1 copy.56
  190.2 1.9 subtract_convert_fusion
  192.1 10.4 %all_gather.3 = bf16[20,16384]{1,0:T(8,128)(2,1)S(1)} all-gather(bf16[20,2048]{1,0:T(8,128)(2,1)S(1)} %get-tuple-element.27), channel_id=1, replica_groups=mesh['dp'=8,'mp'=4] {'dp'}, dimensions={1}, use_global_device_ids=true | all-gather | bytes 737280 | tf_op jit(solution)/shard_map/all_gather | solution.py:148
  202.7 0.9 slice.29
  203.6 1.1 convert_element_type.52
  204.7 0.9 copy.57
  (147 shorter events, 20.2 us)
Async XLA Ops:
  8.0 2.4 %copy-start = (bf16[28,128,128]{2,1,0:T(8,128)(2,1)S(1)}, bf16[28,128,128]{2,1,0:T(8,128)(2,1)}, u32[]{:S(2)}) copy-start(bf16[28,128,128]{2,1,0:T(8,128)(2,1)} %param.13) | copy-start | bytes 2752516
  9.4 11.4 %copy-start.26 = (s32[112]{0:T(128)}, s32[112]{0:T(128)S(1)}, u32[]{:S(2)}) copy-start(s32[112]{0:T(128)S(1)} %get-tuple-element.43) | copy-start | bytes 1348
  10.2 2.1 copy-start.30
  12.3 6.6 %copy-start.11 = (s32[80,2]{0,1:T(2,128)S(1)}, s32[80,2]{0,1:T(2,128)}, u32[]{:S(2)}) copy-start(s32[80,2]{0,1:T(2,128)} %param.16) | copy-start | bytes 1924
  12.3 12.2 %copy-start.7 = (bf16[128,5120]{1,0:T(8,128)(2,1)S(1)}, bf16[128,5120]{1,0:T(8,128)(2,1)}, u32[]{:S(2)}) copy-start(bf16[128,5120]{1,0:T(8,128)(2,1)} %param.11) | copy-start | bytes 3932164
  12.3 29.5 %all-to-all-start = ((bf16[28,128,128]{2,1,0:T(8,128)(2,1)}), bf16[28,128,128]{2,1,0:T(8,128)(2,1)}, u32[]{:S(2)}, u32[]{:S(2)}) async-start(bf16[28,128,128]{2,1,0:T(8,128)(2,1)} %select_select_fusion.1), calls=%async_computation | async-start | bytes 1835008 | tf_op jit(solution)/shard_map/all_to_all | solution.py:66
  20.9 3.6 %copy-start.18 = (s32[20]{0:T(128)}, s32[20]{0:T(128)S(1)}, u32[]{:S(2)}) copy-start(s32[20]{0:T(128)S(1)} %select_reduce_fusion.3) | copy-start | bytes 244
  22.7 1.9 copy-start.23
  26.1 1.6 copy-start.34
  26.1 1.6 copy-start.16
  26.1 1.6 copy-start.27
  26.2 1.7 copy-start.24
  26.2 1.8 copy-start.19
  27.7 16.9 %copy-start.8 = (bf16[20,128,128]{2,1,0:T(8,128)(2,1)S(1)}, bf16[20,128,128]{2,1,0:T(8,128)(2,1)}, u32[]{:S(2)}) copy-start(bf16[20,128,128]{2,1,0:T(8,128)(2,1)} %gather_fusion) | copy-start | bytes 1966084
  27.9 17.1 %copy-start.20 = (pred[20]{0:T(512)(128)(4,1)}, pred[20]{0:T(512)(128)(4,1)S(1)}, u32[]{:S(2)}) copy-start(pred[20]{0:T(512)(128)(4,1)S(1)} %fusion.31) | copy-start | bytes 64
  28.0 15.7 %copy-start.32 = (pred[20]{0:T(512)(128)(4,1)}, pred[20]{0:T(512)(128)(4,1)S(1)}, u32[]{:S(2)}) copy-start(pred[20]{0:T(512)(128)(4,1)S(1)} %and_bitcast_fusion) | copy-start | bytes 64
  47.2 37.2 %all-to-all-start.1 = ((bf16[44,128,128]{2,1,0:T(8,128)(2,1)}), bf16[44,128,128]{2,1,0:T(8,128)(2,1)S(1)}, u32[]{:S(2)}, u32[]{:S(2)}) async-start(bf16[44,128,128]{2,1,0:T(8,128)(2,1)} %select_select_fusion), calls=%async_computation.1 | async-start | bytes 2883584 | tf_op jit(solution)/shard_map/all_to_all | solution.py:93
  50.7 1.4 copy-start.28
  92.7 3.8 %copy-start.25 = (s32[20]{0:T(128)S(1)}, s32[20]{0:T(128)}, u32[]{:S(2)}) copy-start(s32[20]{0:T(128)} %copy-done.23) | copy-start | bytes 244
  92.7 37.4 %all-to-all-start.2 = ((bf16[44,128,128]{2,1,0:T(8,128)(2,1)}), bf16[44,128,128]{2,1,0:T(8,128)(2,1)S(1)}, u32[]{:S(2)}, u32[]{:S(2)}) async-start(bf16[44,128,128]{2,1,0:T(8,128)(2,1)} %copy.53), calls=%async_computation.2 | async-start | bytes 2883584 | tf_op jit(solution)/shard_map/all_to_all | solution.py:117
  96.4 35.2 %copy-start.9 = (bf16[20,128,128]{2,1,0:T(8,128)(2,1)S(1)}, bf16[20,128,128]{2,1,0:T(8,128)(2,1)}, u32[]{:S(2)}) copy-start(bf16[20,128,128]{2,1,0:T(8,128)(2,1)} %gather_fusion) | copy-start | bytes 1966084
  96.4 35.2 %copy-start.22 = (pred[20]{0:T(512)(128)(4,1)S(1)}, pred[20]{0:T(512)(128)(4,1)}, u32[]{:S(2)}) copy-start(pred[20]{0:T(512)(128)(4,1)} %get-tuple-element.30) | copy-start | bytes 64
  96.4 35.2 %copy-start.33 = (pred[20]{0:T(512)(128)(4,1)S(1)}, pred[20]{0:T(512)(128)(4,1)}, u32[]{:S(2)}) copy-start(pred[20]{0:T(512)(128)(4,1)} %copy-done.32) | copy-start | bytes 64
  96.4 93.9 %all-reduce.2.cloned.1.call-start = ((), (), s32[]{:S(2)}) async-start(), calls=%async_computation.7 | async-start | bytes 1572864 | tf_op jit(solution)/shard_map/psum | solution.py:136
  133.2 1.5 copy-start.4
  133.2 1.5 copy-start.10
  133.2 1.5 copy-start.21
  134.7 68.9 %reduce-scatter.2.cloned.1.call-start = ((), (), s32[]{:S(2)}) async-start(), calls=%async_computation.6 | async-start | bytes 3276800 | tf_op jit(solution)/shard_map/reduce_scatter | solution.py:132
  145.7 24.1 %copy-start.17 = (s32[20]{0:T(128)S(1)}, s32[20]{0:T(128)}, u32[]{:S(2)}) copy-start(s32[20]{0:T(128)} %get-tuple-element.33) | copy-start | bytes 244
  146.4 19.8 %all-to-all-start.4 = ((f32[4,7,2048]{2,1,0:T(8,128)}), f32[4,7,2048]{2,1,0:T(8,128)S(1)}, u32[]{:S(2)}, u32[]{:S(2)}) async-start(f32[4,7,2048]{2,1,0:T(8,128)} %all_to_all.31), calls=%async_computation.5 | async-start | bytes 524288 | tf_op jit(solution)/shard_map/all_to_all | solution.py:69
  166.2 21.2 %all-to-all-start.3 = ((f32[4,7,2048]{2,1,0:T(8,128)}), f32[4,7,2048]{2,1,0:T(8,128)S(1)}, u32[]{:S(2)}, u32[]{:S(2)}) async-start(f32[4,7,2048]{2,1,0:T(8,128)} %all_to_all.28), calls=%async_computation.4 | async-start | bytes 524288 | tf_op jit(solution)/shard_map/all_to_all | solution.py:68
  170.5 17.6 %copy-start.5 = (bf16[20,128,128]{2,1,0:T(8,128)(2,1)S(1)}, bf16[20,128,128]{2,1,0:T(8,128)(2,1)}, u32[]{:S(2)}) copy-start(bf16[20,128,128]{2,1,0:T(8,128)(2,1)} %copy-done.3) | copy-start | bytes 1966084
  (10 other events, 8.9 us)
Sparse Core Ops, SparseCore 0:
  134.8 54.8 all-reduce.1
Sparse Core Ops, SparseCore 1:
  143.4 59.5 reduce-scatter.1
where the time goes:
time: 214 us; the launch traced here: 213 us
  waiting for transfers between devices  111 us (52%)
  local copies, waits for them, and re-layouts  28.9 us (14%)
  starting transfers between devices  20.8 us (10%)
  other arithmetic  18.8 us (9%)
  between operations  16.2 us (8%)
  blocking collectives  10.4 us (5%)
  matrix products  6.59 us (3%)
    all_to_all x1, waiting for transfers between devices, body(): lax.all_to_all(outgoing_slopes, 'mp', split_axis=0, concat_axis=0, tiled=...  33.6 us
    all_to_all x1, waiting for transfers between devices, body(): lax.all_to_all(outgoing_products, 'mp', split_axis=0, concat_axis=0, tile...  32 us
    all_to_all x1, waiting for transfers between devices, body(): lax.all_to_all(out_first, 'mp', split_axis=0, concat_axis=0, tiled=True)  16.9 us
    all_to_all x1, waiting for transfers between devices, body(): lax.all_to_all(out_second, 'mp', split_axis=0, concat_axis=0, tiled=True)  15.6 us
    all_to_all x1, waiting for transfers between devices, body(): lax.all_to_all(outgoing, 'mp', split_axis=0, concat_axis=0, tiled=True)  13.3 us
    all_gather x1, blocking collectives, body(): lax.all_gather(weight_next, 'dp', axis=1, tiled=True)  10.4 us
    unnamed x79, local copies, waits for them, and re-layouts  8.8 us
    all_to_all x1, starting transfers between devices, body(): lax.all_to_all(outgoing, 'mp', split_axis=0, concat_axis=0, tiled=True)  6.48 us
  transfers between devices with their start and end apart: 7, of which 5 were waited for; matrix products, arithmetic and copies ran while one was open for 13% of the time, Pallas kernels for 0%

commit v1 on v0

--- a/solution.py
+++ b/solution.py
@@ -114,7 +114,15 @@
     outgoing_slopes = jnp.einsum(
         "qc,tcn->qtn", placement, band_slopes, preferred_element_type=jnp.float32
     ).astype(jnp.bfloat16)
-    arrived_slopes = lax.all_to_all(outgoing_slopes, "mp", split_axis=0, concat_axis=0, tiled=True)
+    ways, here = (lax.axis_size("mp"), lax.axis_index("mp"))
+    width = outgoing_slopes.shape[0] // ways
+    turned = jnp.roll(outgoing_slopes, -here * width, axis=0)
+    got = [lax.slice_in_dim(turned, 0, width, axis=0)]
+    for far in range(1, ways):
+        sent = lax.slice_in_dim(turned, far * width, (far + 1) * width, axis=0)
+        got.append(lax.ppermute(sent, "mp", [(d, (d + far) % ways) for d in range(ways)]))
+    line = jnp.concatenate(got[::-1], axis=0)
+    arrived_slopes = jnp.roll(line, (here + 1) * got[0].shape[0], axis=0)
     slope_blocks = jnp.take(arrived_slopes, out_place, axis=0)
     slope_form = "btn"
     block_grads = jnp.einsum(

time: 214 us -> 233 us (1.089)
  starting transfers between devices: 20.8 us -> 30 us
  other arithmetic: 18.8 us -> 25.9 us
    ppermute x0 -> x3, waiting for transfers between devices: none -> 33.7 us  [body(): lax.ppermute(sent, 'mp', [(d, (d + far) % ways) for d in range(ways)])]
    all_to_all x1 -> x0, waiting for transfers between devices: 33.6 us -> none  [body(): lax.all_to_all(outgoing_slopes, 'mp', split_axis=0, concat_axis=0, tiled=...]
    all_to_all x1, starting transfers between devices: 3.43 us -> 12.1 us  [body(): lax.all_to_all(out_second, 'mp', split_axis=0, concat_axis=0, tiled=True)]
    concatenate x0 -> x2, other arithmetic: none -> 6.9 us  [the longest x1 5.54 us: body(): arrived_slopes = jnp.roll(line, (here + 1) * got[0].shape[0], axis=0)]
    ppermute x0 -> x3, starting transfers between devices: none -> 3.83 us  [body(): lax.ppermute(sent, 'mp', [(d, (d + far) % ways) for d in range(ways)])]
    all_to_all x1 -> x0, starting transfers between devices: 3.68 us -> none  [body(): lax.all_to_all(outgoing_slopes, 'mp', split_axis=0, concat_axis=0, tiled=...]
    unnamed x79 -> x77, local copies, waits for them, and re-layouts: 8.8 us -> 8.8 us
  transfers between devices with their start and end apart: 7 -> 9, of which waited for: 5 -> 8; matrix products, arithmetic and copies ran while one was open for 13% -> 12% of each run, Pallas kernels for 0% -> 0%
where the time goes in v1:
time: 233 us; the launch traced here: 232 us
  waiting for transfers between devices  112 us (48%)
  local copies, waits for them, and re-layouts  30.5 us (13%)
  starting transfers between devices  30 us (13%)
  other arithmetic  25.9 us (11%)
  between operations  16.2 us (7%)
  blocking collectives  9.53 us (4%)
  matrix products  7.7 us (3%)
    ppermute x3, waiting for transfers between devices, body(): lax.ppermute(sent, 'mp', [(d, (d + far) % ways) for d in range(ways)])  33.7 us
    all_to_all x1, waiting for transfers between devices, body(): lax.all_to_all(outgoing_products, 'mp', split_axis=0, concat_axis=0, tile...  31.9 us
    all_to_all x1, waiting for transfers between devices, body(): lax.all_to_all(out_second, 'mp', split_axis=0, concat_axis=0, tiled=True)  15.9 us
    all_to_all x1, waiting for transfers between devices, body(): lax.all_to_all(out_first, 'mp', split_axis=0, concat_axis=0, tiled=True)  14.8 us
    all_to_all x1, waiting for transfers between devices, body(): lax.all_to_all(outgoing, 'mp', split_axis=0, concat_axis=0, tiled=True)  13.3 us
    all_to_all x1, starting transfers between devices, body(): lax.all_to_all(out_second, 'mp', split_axis=0, concat_axis=0, tiled=True)  12.1 us
    all_gather x1, blocking collectives, body(): lax.all_gather(weight_next, 'dp', axis=1, tiled=True)  9.53 us
    unnamed x77, local copies, waits for them, and re-layouts  8.8 us
  transfers between devices with their start and end apart: 9, of which 8 were waited for; matrix products, arithmetic and copies ran while one was open for 12% of the time, Pallas kernels for 0%

profile of v1, /device:TPU:0, one launch (start us, length us, event | category | flops | bytes accessed | tf_op | source)
XLA Modules:
  0.0 231.9 jit_solution(16139799399601016081)
XLA Ops:
  12.3 6.5 %all-to-all-start = ((bf16[28,128,128]{2,1,0:T(8,128)(2,1)}), bf16[28,128,128]{2,1,0:T(8,128)(2,1)}, u32[]{:S(2)}, u32[]{:S(2)}) async-start(bf16[28,128,128]{2,1,0:T(8,128)(2,1)} %select_select_fusion.1), calls=%async_computation | async-start | bytes 1835008 | tf_op jit(solution)/shard_map/all_to_all | solution.py:66
  26.2 1.5 gather_fusion
  28.6 13.3 %all-to-all-done = bf16[28,128,128]{2,1,0:T(8,128)(2,1)} async-done(((bf16[28,128,128]{2,1,0:T(8,128)(2,1)}), bf16[28,128,128]{2,1,0:T(8,128)(2,1)}, u32[]{:S(2)}, u32[]{:S(2)}) %all-to-all-start) | async-done | bytes 917536 | tf_op jit(solution)/shard_map/all_to_all | solution.py:66
  41.8 1.8 gather_fusion.3
  44.5 1.5 convolution_convert_fusion.2
  48.3 3.7 %all-to-all-start.1 = ((bf16[44,128,128]{2,1,0:T(8,128)(2,1)}), bf16[44,128,128]{2,1,0:T(8,128)(2,1)S(1)}, u32[]{:S(2)}, u32[]{:S(2)}) async-start(bf16[44,128,128]{2,1,0:T(8,128)(2,1)} %select_select_fusion), calls=%async_computation.1 | async-start | bytes 2883584 | tf_op jit(solution)/shard_map/all_to_all | solution.py:93
  52.0 1.4 copy.51
  53.7 31.9 %all-to-all-done.1 = bf16[44,128,128]{2,1,0:T(8,128)(2,1)S(1)} async-done(((bf16[44,128,128]{2,1,0:T(8,128)(2,1)}), bf16[44,128,128]{2,1,0:T(8,128)(2,1)S(1)}, u32[]{:S(2)}, u32[]{:S(2)}) %all-to-all-start.1) | async-done | bytes 1441824 | tf_op jit(solution)/shard_map/all_to_all | solution.py:93
  85.6 2.1 fusion.10
  87.7 1.8 copy.50
  89.5 2.1 fusion.15
  91.6 1.5 copy.52
  93.7 1.4 fusion.7
  95.1 1.6 fusion.60
  96.7 2.0 collective-permute-start.1
  98.7 1.8 collective-permute-start
  100.5 13.1 %collective-permute-done.2 = bf16[11,128,128]{2,0,1:T(8,128)(2,1)S(1)} collective-permute-done((bf16[11,128,128]{2,0,1:T(8,128)(2,1)}, bf16[11,128,128]{2,0,1:T(8,128)(2,1)S(1)}, u32[]{:S(2)}, u32[]{:S(2)}) %collective-permute-start.2) | collective-permute-done | bytes 360480 | tf_op jit(solution)/shard_map/ppermute | solution.py:123
  113.6 20.6 %collective-permute-done.1 = bf16[11,128,128]{2,0,1:T(8,128)(2,1)S(1)} collective-permute-done((bf16[11,128,128]{2,0,1:T(8,128)(2,1)}, bf16[11,128,128]{2,0,1:T(8,128)(2,1)S(1)}, u32[]{:S(2)}, u32[]{:S(2)}) %collective-permute-start.1) | collective-permute-done | bytes 360480 | tf_op jit(solution)/shard_map/ppermute | solution.py:123
  134.2 5.5 %fusion.3 = bf16[44,128,128]{2,0,1:T(8,128)(2,1)S(1)} fusion(s32[]{:T(128)S(6)} %select_n.302, bf16[11,128,128]{2,0,1:T(8,128)(2,1)S(1)} %collective-permute-done, bf16[11,128,128]{2,0,1:T(8,128)(2,1)S(1)} %collective-permute-done.1, bf16[11,128,128]{2,0,1:T(8,128)(2,1)S(1)} %collective-permute-done.2, bf16[11,128,128]{2,0,1:T(8,128)(2,1)S(1)} %get-tuple-element.39), kind=kLoop, calls=%fused_computation.29 | loop fusion | flops 11534336 | bytes 2883588 | tf_op jit(solution)/shard_map/jit(_roll_dynamic)/concatenate | solution.py:125
  140.2 1.5 gather_fusion.5
  141.7 1.6 convolution_convert_fusion.1
  143.4 1.4 copy.60
  144.9 1.7 fusion.27
  146.9 4.4 %scatter_fusion = f32[128,40,128]{2,0,1:T(8,128)S(1)} fusion(f32[128,40,128]{2,0,1:T(8,128)S(1)} %broadcast_in_dim.224, s32[20]{0:T(128)S(1)} %get-tuple-element.53, f32[20,128,128]{2,1,0:T(8,128)} %fusion.27), kind=kCustom, calls=%fused_computation.10 | custom fusion | flops 327680 | bytes 3932240 | tf_op jit(solution)/shard_map/scatter-add | solution.py:138
  151.3 2.1 copy.54
  156.6 12.1 %all-to-all-start.3 = ((f32[4,7,2048]{2,1,0:T(8,128)}), f32[4,7,2048]{2,1,0:T(8,128)S(1)}, u32[]{:S(2)}, u32[]{:S(2)}) async-start(f32[4,7,2048]{2,1,0:T(8,128)} %all_to_all.27), calls=%async_computation.4 | async-start | bytes 524288 | tf_op jit(solution)/shard_map/all_to_all | solution.py:69
  169.4 15.9 %all-to-all-done.3 = f32[4,7,2048]{2,1,0:T(8,128)S(1)} async-done(((f32[4,7,2048]{2,1,0:T(8,128)}), f32[4,7,2048]{2,1,0:T(8,128)S(1)}, u32[]{:S(2)}, u32[]{:S(2)}) %all-to-all-start.3) | async-done | bytes 229408 | tf_op jit(solution)/shard_map/all_to_all | solution.py:69
  185.3 3.8 %all-to-all-start.2 = ((f32[4,7,2048]{2,1,0:T(8,128)}), f32[4,7,2048]{2,1,0:T(8,128)S(1)}, u32[]{:S(2)}, u32[]{:S(2)}) async-start(f32[4,7,2048]{2,1,0:T(8,128)} %all_to_all.24), calls=%async_computation.3 | async-start | bytes 524288 | tf_op jit(solution)/shard_map/all_to_all | solution.py:68
  189.9 14.8 %all-to-all-done.2 = f32[4,7,2048]{2,1,0:T(8,128)S(1)} async-done(((f32[4,7,2048]{2,1,0:T(8,128)}), f32[4,7,2048]{2,1,0:T(8,128)S(1)}, u32[]{:S(2)}, u32[]{:S(2)}) %all-to-all-start.2) | async-done | bytes 229408 | tf_op jit(solution)/shard_map/all_to_all | solution.py:68
  207.5 1.7 all-reduce.2.cloned.1.call-done
  209.2 1.9 subtract_convert_fusion
  211.1 9.5 %all_gather.3 = bf16[20,16384]{1,0:T(8,128)(2,1)S(1)} all-gather(bf16[20,2048]{1,0:T(8,128)(2,1)S(1)} %get-tuple-element.28), channel_id=1, replica_groups=mesh['dp'=8,'mp'=4] {'dp'}, dimensions={1}, use_global_device_ids=true | all-gather | bytes 737280 | tf_op jit(solution)/shard_map/all_gather | solution.py:156
  (152 shorter events, 28.3 us)
Async XLA Ops:
  8.0 2.4 %copy-start = (bf16[28,128,128]{2,1,0:T(8,128)(2,1)S(1)}, bf16[28,128,128]{2,1,0:T(8,128)(2,1)}, u32[]{:S(2)}) copy-start(bf16[28,128,128]{2,1,0:T(8,128)(2,1)} %param.15) | copy-start | bytes 2752516
  9.4 11.3 %copy-start.26 = (s32[112]{0:T(128)}, s32[112]{0:T(128)S(1)}, u32[]{:S(2)}) copy-start(s32[112]{0:T(128)S(1)} %get-tuple-element.48) | copy-start | bytes 1348
  10.3 2.0 copy-start.11
  10.4 2.0 copy-start.13
  11.1 7.8 %copy-start.10 = (s32[80,2]{0,1:T(2,128)S(1)}, s32[80,2]{0,1:T(2,128)}, u32[]{:S(2)}) copy-start(s32[80,2]{0,1:T(2,128)} %param.18) | copy-start | bytes 1924
  12.3 12.2 %copy-start.7 = (bf16[128,5120]{1,0:T(8,128)(2,1)S(1)}, bf16[128,5120]{1,0:T(8,128)(2,1)}, u32[]{:S(2)}) copy-start(bf16[128,5120]{1,0:T(8,128)(2,1)} %param.13) | copy-start | bytes 3932164
  12.3 29.5 %all-to-all-start = ((bf16[28,128,128]{2,1,0:T(8,128)(2,1)}), bf16[28,128,128]{2,1,0:T(8,128)(2,1)}, u32[]{:S(2)}, u32[]{:S(2)}) async-start(bf16[28,128,128]{2,1,0:T(8,128)(2,1)} %select_select_fusion.1), calls=%async_computation | async-start | bytes 1835008 | tf_op jit(solution)/shard_map/all_to_all | solution.py:66
  20.9 3.6 %copy-start.17 = (s32[20]{0:T(128)}, s32[20]{0:T(128)S(1)}, u32[]{:S(2)}) copy-start(s32[20]{0:T(128)S(1)} %select_reduce_fusion.3) | copy-start | bytes 244
  22.6 1.9 copy-start.22
  26.1 1.7 copy-start.23
  26.1 1.8 copy-start.18
  27.8 18.2 %copy-start.19 = (pred[20]{0:T(512)(128)(4,1)}, pred[20]{0:T(512)(128)(4,1)S(1)}, u32[]{:S(2)}) copy-start(pred[20]{0:T(512)(128)(4,1)S(1)} %fusion.39) | copy-start | bytes 64
  28.0 18.1 %copy-start.31 = (pred[20]{0:T(512)(128)(4,1)}, pred[20]{0:T(512)(128)(4,1)S(1)}, u32[]{:S(2)}) copy-start(pred[20]{0:T(512)(128)(4,1)S(1)} %and_bitcast_fusion) | copy-start | bytes 64
  48.3 5.2 %copy-start.25 = (s32[80]{0:T(128)S(1)}, s32[80]{0:T(128)}, u32[]{:S(2)}) copy-start(s32[80]{0:T(128)} %get-tuple-element.47) | copy-start | bytes 964
  48.3 5.2 %copy-start.28 = (s32[80]{0:T(128)S(1)}, s32[80]{0:T(128)}, u32[]{:S(2)}) copy-start(s32[80]{0:T(128)} %get-tuple-element.35) | copy-start | bytes 964
  48.3 37.4 %all-to-all-start.1 = ((bf16[44,128,128]{2,1,0:T(8,128)(2,1)}), bf16[44,128,128]{2,1,0:T(8,128)(2,1)S(1)}, u32[]{:S(2)}, u32[]{:S(2)}) async-start(bf16[44,128,128]{2,1,0:T(8,128)(2,1)} %select_select_fusion), calls=%async_computation.1 | async-start | bytes 2883584 | tf_op jit(solution)/shard_map/all_to_all | solution.py:93
  51.9 157.2 %all-reduce.2.cloned.1.call-start = ((), (), s32[]{:S(2)}) async-start(), calls=%async_computation.6 | async-start | bytes 1572864 | tf_op jit(solution)/shard_map/psum | solution.py:144
  95.1 5.5 %copy-start.24 = (s32[20]{0:T(128)S(1)}, s32[20]{0:T(128)}, u32[]{:S(2)}) copy-start(s32[20]{0:T(128)} %copy-done.22) | copy-start | bytes 244
  96.7 16.9 %collective-permute-start.2 = (bf16[11,128,128]{2,0,1:T(8,128)(2,1)}, bf16[11,128,128]{2,0,1:T(8,128)(2,1)S(1)}, u32[]{:S(2)}, u32[]{:S(2)}) collective-permute-start(bf16[11,128,128]{2,0,1:T(8,128)(2,1)} %get-tuple-element.40), channel_id=1, source_target_pairs={{0,1},{1,2},{2,3},{3,0},{4,5},{5,6},{6,7},{7,4},{8,9},{9,10},{10,1... | collective-permute-start | bytes 1081352 | tf_op jit(solution)/shard_map/ppermute | solution.py:123
  96.7 37.6 %collective-permute-start.1 = (bf16[11,128,128]{2,0,1:T(8,128)(2,1)}, bf16[11,128,128]{2,0,1:T(8,128)(2,1)S(1)}, u32[]{:S(2)}, u32[]{:S(2)}) collective-permute-start(bf16[11,128,128]{2,0,1:T(8,128)(2,1)} %get-tuple-element.41), channel_id=1, source_target_pairs={{0,2},{1,3},{2,0},{3,1},{4,6},{5,7},{6,4},{7,5},{8,10},{9,11},{10,... | collective-permute-start | bytes 1081352 | tf_op jit(solution)/shard_map/ppermute | solution.py:123
  98.7 35.5 %collective-permute-start = (bf16[11,128,128]{2,0,1:T(8,128)(2,1)S(1)}, bf16[11,128,128]{2,0,1:T(8,128)(2,1)S(1)}, u32[]{:S(2)}, u32[]{:S(2)}) collective-permute-start(bf16[11,128,128]{2,0,1:T(8,128)(2,1)S(1)} %get-tuple-element.42), channel_id=1, source_target_pairs={{0,3},{1,0},{2,1},{3,2},{4,7},{5,4},{6,5},{7,6},{8,11},{9,8},{10,9... | collective-permute-start | bytes 1081352 | tf_op jit(solution)/shard_map/ppermute | solution.py:123
  139.8 1.9 copy-start.8
  139.8 1.9 copy-start.21
  139.8 1.9 copy-start.32
  143.3 1.6 copy-start.4
  143.3 1.6 copy-start.9
  143.3 1.6 copy-start.20
  144.8 77.6 %reduce-scatter.2.cloned.1.call-start = ((), (), s32[]{:S(2)}) async-start(), calls=%async_computation.5 | async-start | bytes 3276800 | tf_op jit(solution)/shard_map/reduce_scatter | solution.py:140
  155.7 33.4 %copy-start.16 = (s32[20]{0:T(128)S(1)}, s32[20]{0:T(128)}, u32[]{:S(2)}) copy-start(s32[20]{0:T(128)} %get-tuple-element.34) | copy-start | bytes 244
  156.6 28.7 %all-to-all-start.3 = ((f32[4,7,2048]{2,1,0:T(8,128)}), f32[4,7,2048]{2,1,0:T(8,128)S(1)}, u32[]{:S(2)}, u32[]{:S(2)}) async-start(f32[4,7,2048]{2,1,0:T(8,128)} %all_to_all.27), calls=%async_computation.4 | async-start | bytes 524288 | tf_op jit(solution)/shard_map/all_to_all | solution.py:69
  185.3 19.3 %all-to-all-start.2 = ((f32[4,7,2048]{2,1,0:T(8,128)}), f32[4,7,2048]{2,1,0:T(8,128)S(1)}, u32[]{:S(2)}, u32[]{:S(2)}) async-start(f32[4,7,2048]{2,1,0:T(8,128)} %all_to_all.24), calls=%async_computation.3 | async-start | bytes 524288 | tf_op jit(solution)/shard_map/all_to_all | solution.py:68
  189.8 15.4 %copy-start.5 = (bf16[20,128,128]{2,1,0:T(8,128)(2,1)S(1)}, bf16[20,128,128]{2,1,0:T(8,128)(2,1)}, u32[]{:S(2)}) copy-start(bf16[20,128,128]{2,1,0:T(8,128)(2,1)} %copy-done.3) | copy-start | bytes 1966084
  (11 other events, 11.5 us)
Sparse Core Ops, SparseCore 0:
  144.9 64.1 all-reduce.1
Sparse Core Ops, SparseCore 1:
  153.6 68.8 reduce-scatter.1
